TPU v7x, 32 devices: a whole 2x2x4 slice. The times are simulated.
32 devices in a mesh: src: 4 (over z), delay: 8 (over y, x, core).
Axes of the slice: x: 2, y: 2, z: 4, core: 2. Of those that a mesh axis runs over, the one named last changes fastest.
Arguments:
- history: float32 [32, 16, 16, 128], P('delay', 'src'), may hold values from -6 to 6
- slot_map: int32 [32], P('delay'), may hold values from 0 to 3, as said below
- interaction: float32 [1536, 128, 128], P(('src', 'delay')), may hold values from -0.0546875 to 0.0546875
- pattern: int32 [3, 1536], P(None, ('src', 'delay')), may hold values from 0 to 15, as said below
- live: int32 [32], P(('src', 'delay')), may hold values from 12 to 48
- near_inverse: float32 [16, 128, 128], P('src'), may hold values from -0.5 to 0.5
- incident: float32 [4, 16, 16, 128], P(None, 'src'), may hold values from -6 to 6
Outputs:
- currents: float32 [4, 16, 16, 128], P(None, 'src')
Inputs may be any that keep to these rules, and one draw needn't show every extreme that they name: `slot_map`: each band's 4 entries are a cyclic rotation of 0 .. 3. `pattern`: row 0 lies in 0 .. 3, row 1 in 0 .. 15, row 2 in 0 .. 3.
All inputs are finite; a program needn't handle non-finite values.
Results may differ from a plain program's by a relative error of at most 0.0003.
Values sent between devices are 32-bit elements; how exact they have to be, the bound alone decides.
No kernel may reach another device: no remote copies, remote signals or barrier semaphores. Data moves between devices by JAX's collectives and lax.ppermute only.
A program may use at most 64 MiB of HBM per device.

v0:
```python
import jax
import jax.numpy as jnp
from jax import lax
from jax.sharding import PartitionSpec as P


def shifted(x, axis, by):
    devices = lax.axis_size(axis)
    pairs = [(i, i + by) for i in range(devices) if 0 <= i + by < devices]
    return lax.ppermute(x, axis, pairs)


def slot_holding(slot_map, wanted, moment):
    length = slot_map.shape[0]
    positions = jnp.arange(length, dtype=jnp.int32)
    return jnp.sum(jnp.where((slot_map + moment) % length == wanted, positions, 0))


def body(history, slot_map, interaction, pattern, live, near_inverse, incident):
    slot_count = history.shape[0]
    group_blocks = history.shape[1]
    columns = history.shape[2]
    block_width = history.shape[3]
    moments = incident.shape[0]
    pair_count = interaction.shape[0]
    positions = jnp.arange(slot_count, dtype=jnp.int32)
    at_front = lax.axis_index("delay") == 0
    in_use = (jnp.arange(pair_count, dtype=jnp.int32) < live[0]).astype(jnp.float32)
    row_match = pattern[0][None, :] == jnp.arange(group_blocks, dtype=jnp.int32)[:, None]
    selector = row_match.astype(jnp.float32) * in_use[None, :]
    band_state = lax.all_gather(history, "src", axis=1, tiled=True)
    results = []
    newest = None
    for moment in range(moments):
        if moment > 0:
            vacated = slot_holding(slot_map, slot_count - 1, moment - 1)
            outgoing_slot = lax.dynamic_index_in_dim(band_state, vacated, 0, keepdims=False)
            incoming = shifted(outgoing_slot, "delay", 1)
            entering = jnp.where(at_front, newest, incoming)
            band_state = lax.dynamic_update_index_in_dim(band_state, entering, vacated, 0)
        holder_match = (slot_map[None, :] + moment) % slot_count == pattern[2][:, None]
        holder = jnp.sum(jnp.where(holder_match, positions[None, :], 0), axis=1)
        picked = band_state[holder, pattern[1]]
        products = jnp.einsum("pab,prb->pra", interaction, picked, precision=lax.Precision.HIGHEST)
        partial_field = jnp.dot(
            selector,
            products.reshape(pair_count, columns * block_width),
            precision=lax.Precision.HIGHEST,
        )
        partial_field = partial_field.reshape(group_blocks, columns, block_width)
        field_sum = lax.psum(partial_field, "delay")
        current = jnp.einsum(
            "iab,irb->ira",
            near_inverse,
            incident[moment] - field_sum,
            precision=lax.Precision.HIGHEST,
        )
        results.append(current)
        if moment + 1 < moments:
            newest = lax.all_gather(current, "src", axis=0, tiled=True)
    return jnp.stack(results)


def solution(mesh):
    return jax.shard_map(
        body,
        mesh=mesh,
        in_specs=(
            P("delay", "src", None, None),
            P("delay"),
            P(("src", "delay"), None, None),
            P(None, ("src", "delay")),
            P(("src", "delay")),
            P("src", None, None),
            P(None, "src", None, None),
        ),
        out_specs=P(None, "src", None, None),
        check_vma=False,
    )
```

profile of v0, /device:TPU:4, one launch (start us, length us, event | category | flops | bytes accessed | tf_op | source)
XLA Modules:
  0.0 216.7 jit_solution(3523601571943106550)
XLA Ops:
  0.0 1.5 fusion.45
  1.5 18.1 %all_gather.12 = f32[4,16,16,128]{3,2,1,0:T(8,128)} all-gather(f32[4,4,16,128]{3,2,1,0:T(8,128)} %param.7), channel_id=1, replica_groups=mesh['src'=4,'delay'=8] {'src'}, dimensions={1}, use_global_device_ids=true | all-gather | bytes 655360 | tf_op jit(solution)/shard_map/all_gather | solution.py:31
  21.5 1.6 dynamic-slice_bitcast_fusion.2
  23.1 1.9 collective-permute-start
  25.0 0.8 slice_bitcast_fusion.1
  25.9 0.7 fusion.64
  26.6 2.6 %gather_fusion = f32[48,16,128]{2,1,0:T(8,128)} fusion(f32[4,16,16,128]{3,2,1,0:T(8,128)} %all_gather.12, s32[48]{0:T(128)S(1)} %get-tuple-element.25), kind=kCustom, calls=%fused_computation | custom fusion | bytes 786816 | tf_op jit(solution)/shard_map/gather | solution.py:43
  29.9 6.0 %fusion.74 = f32[48,16,128]{2,1,0:T(8,128)S(1)} fusion(f32[48,16,128]{2,1,0:T(8,128)} %gather_fusion, f32[48,128,128]{2,1,0:T(8,128)S(1)} %copy-done), kind=kOutput, calls=%fused_computation.121 | convolution fusion | flops 150994944 | bytes 3932160 | tf_op jit(solution)/shard_map/pab,prb->pra/dot_general | solution.py:44
  36.3 24.8 %psum.28 = f32[4,16,128]{2,0,1:T(4,128)S(1)} all-reduce(f32[4,16,128]{2,0,1:T(4,128)S(1)} %fusion.9), channel_id=1, replica_groups=mesh['src'=4,'delay'=8] {'delay'}, use_global_device_ids=true, to_apply=%region_1.2 | all-reduce | flops 8192 | bytes 65536 | tf_op jit(solution)/shard_map/psum | solution.py:51
  61.1 1.4 fusion.73
  66.7 13.4 %all_gather.13 = f32[16,16,128]{2,1,0:T(8,128)S(1)} all-gather(f32[4,16,128]{2,1,0:T(8,128)S(1)} %fusion.21), channel_id=1, replica_groups=mesh['src'=4,'delay'=8] {'src'}, dimensions={0}, use_global_device_ids=true | all-gather | bytes 163840 | tf_op jit(solution)/shard_map/all_gather | solution.py:60
  80.0 1.6 bitcast_dynamic-update-slice_fusion.2
  81.6 2.6 %gather_fusion.1 = f32[48,16,128]{2,1,0:T(8,128)} fusion(f32[4,16,16,128]{3,2,1,0:T(8,128)} %bitcast_dynamic-update-slice_fusion.2, s32[48]{0:T(128)S(1)} %get-tuple-element.24), kind=kCustom, calls=%fused_computation.1 | custom fusion | bytes 786816 | tf_op jit(solution)/shard_map/gather | solution.py:43
  84.3 6.0 %fusion.75 = f32[48,16,128]{2,1,0:T(8,128)S(1)} fusion(f32[48,16,128]{2,1,0:T(8,128)} %gather_fusion.1, f32[48,128,128]{2,1,0:T(8,128)S(1)} %copy-done), kind=kOutput, calls=%fused_computation.122 | convolution fusion | flops 150994944 | bytes 3932160 | tf_op jit(solution)/shard_map/pab,prb->pra/dot_general | solution.py:44
  90.2 1.0 fusion.6
  91.3 22.9 %psum.29 = f32[4,16,128]{2,0,1:T(4,128)S(1)} all-reduce(f32[4,16,128]{2,0,1:T(4,128)} %fusion.6), channel_id=1, replica_groups=mesh['src'=4,'delay'=8] {'delay'}, use_global_device_ids=true, to_apply=%region_4.5 | all-reduce | flops 8192 | bytes 65536 | tf_op jit(solution)/shard_map/psum | solution.py:51
  114.2 0.9 dynamic-slice_bitcast_fusion.1
  115.1 1.9 collective-permute-start.1
  117.6 13.9 %all_gather.14 = f32[16,16,128]{2,1,0:T(8,128)S(1)} all-gather(f32[4,16,128]{2,1,0:T(8,128)S(1)} %fusion.19), channel_id=1, replica_groups=mesh['src'=4,'delay'=8] {'src'}, dimensions={0}, use_global_device_ids=true | all-gather | bytes 163840 | tf_op jit(solution)/shard_map/all_gather | solution.py:60
  132.1 2.6 %gather_fusion.2 = f32[48,16,128]{2,1,0:T(8,128)} fusion(f32[4,16,16,128]{3,2,1,0:T(8,128)} %bitcast_dynamic-update-slice_fusion.1, s32[48]{0:T(128)S(1)} %get-tuple-element.23), kind=kCustom, calls=%fused_computation.2 | custom fusion | bytes 786816 | tf_op jit(solution)/shard_map/gather | solution.py:43
  134.7 6.0 %fusion.76 = f32[48,16,128]{2,1,0:T(8,128)S(1)} fusion(f32[48,16,128]{2,1,0:T(8,128)} %gather_fusion.2, f32[48,128,128]{2,1,0:T(8,128)S(1)} %copy-done), kind=kOutput, calls=%fused_computation.123 | convolution fusion | flops 150994944 | bytes 3932160 | tf_op jit(solution)/shard_map/pab,prb->pra/dot_general | solution.py:44
  140.7 1.0 fusion.3
  141.7 22.9 %psum.30 = f32[4,16,128]{2,0,1:T(4,128)S(1)} all-reduce(f32[4,16,128]{2,0,1:T(4,128)} %fusion.3), channel_id=1, replica_groups=mesh['src'=4,'delay'=8] {'delay'}, use_global_device_ids=true, to_apply=%region_7.8 | all-reduce | flops 8192 | bytes 65536 | tf_op jit(solution)/shard_map/psum | solution.py:51
  164.6 0.9 dynamic-slice_bitcast_fusion
  165.6 1.9 collective-permute-start.2
  168.0 13.5 %all_gather.15 = f32[16,16,128]{2,1,0:T(8,128)S(1)} all-gather(f32[4,16,128]{2,1,0:T(8,128)S(1)} %fusion.17), channel_id=1, replica_groups=mesh['src'=4,'delay'=8] {'src'}, dimensions={0}, use_global_device_ids=true | all-gather | bytes 163840 | tf_op jit(solution)/shard_map/all_gather | solution.py:60
  182.2 2.6 %gather_fusion.3 = f32[48,16,128]{2,1,0:T(8,128)} fusion(f32[4,16,16,128]{3,2,1,0:T(8,128)} %bitcast_dynamic-update-slice_fusion, s32[48]{0:T(128)S(1)} %get-tuple-element.9), kind=kCustom, calls=%fused_computation.3 | custom fusion | bytes 786816 | tf_op jit(solution)/shard_map/gather | solution.py:43
  184.9 6.0 %fusion.77 = f32[48,16,128]{2,1,0:T(8,128)S(1)} fusion(f32[48,16,128]{2,1,0:T(8,128)} %gather_fusion.3, f32[48,128,128]{2,1,0:T(8,128)S(1)} %copy-done), kind=kOutput, calls=%fused_computation.124 | convolution fusion | flops 150994944 | bytes 3932160 | tf_op jit(solution)/shard_map/pab,prb->pra/dot_general | solution.py:44
  190.8 1.0 fusion
  191.9 22.9 %psum.31 = f32[4,16,128]{2,0,1:T(4,128)S(1)} all-reduce(f32[4,16,128]{2,0,1:T(4,128)} %fusion), channel_id=1, replica_groups=mesh['src'=4,'delay'=8] {'delay'}, use_global_device_ids=true, to_apply=%region_10.11 | all-reduce | flops 8192 | bytes 65536 | tf_op jit(solution)/shard_map/psum | solution.py:51
  214.8 0.8 fusion.12
  216.0 0.7 pad_maximum_fusion
  (26 shorter events, 3.9 us)
Async XLA Ops:
  0.0 29.9 %copy-start = (f32[48,128,128]{2,1,0:T(8,128)S(1)}, f32[48,128,128]{2,1,0:T(8,128)}, u32[]{:S(2)}) copy-start(f32[48,128,128]{2,1,0:T(8,128)} %param.9) | copy-start | bytes 9437188
  1.5 61.0 %copy-start.1 = (f32[4,128,128]{2,1,0:T(8,128)S(1)}, f32[4,128,128]{2,1,0:T(8,128)}, u32[]{:S(2)}) copy-start(f32[4,128,128]{2,1,0:T(8,128)} %param.12) | copy-start | bytes 786436
  23.1 56.9 %collective-permute-start = (f32[16,16,128]{2,1,0:T(8,128)}, f32[16,16,128]{2,1,0:T(8,128)}, u32[]{:S(2)}, u32[]{:S(2)}) collective-permute-start(f32[16,16,128]{2,1,0:T(8,128)} %dynamic-slice_bitcast_fusion.2), channel_id=1, source_target_pairs={{0,1},{1,2},{2,3},{3,4},{4,5},{5,6},{6,7},{8,9},{9,10},{10,11},{11... | collective-permute-start | bytes 393224 | tf_op jit(solution)/shard_map/ppermute | solution.py:10
  29.9 6.0 %copy-start.2 = (f32[48]{0:T(128)}, f32[48]{0:T(128)S(1)}, u32[]{:S(2)}) copy-start(f32[48]{0:T(128)S(1)} %compare_convert_fusion) | copy-start | bytes 580
  62.5 27.7 %copy-start.3 = (f32[48]{0:T(128)S(1)}, f32[48]{0:T(128)}, u32[]{:S(2)}) copy-start(f32[48]{0:T(128)} %copy-done.2) | copy-start | bytes 580
  90.2 50.5 %copy-start.4 = (f32[48]{0:T(128)S(1)}, f32[48]{0:T(128)}, u32[]{:S(2)}) copy-start(f32[48]{0:T(128)} %copy-done.2) | copy-start | bytes 580
  115.1 16.3 %collective-permute-start.1 = (f32[16,16,128]{2,1,0:T(8,128)S(1)}, f32[16,16,128]{2,1,0:T(8,128)S(1)}, u32[]{:S(2)}, u32[]{:S(2)}) collective-permute-start(f32[16,16,128]{2,1,0:T(8,128)S(1)} %dynamic-slice_bitcast_fusion.1), channel_id=1, source_target_pairs={{0,1},{1,2},{2,3},{3,4},{4,5},{5,6},{6,7},{8,9},{9,10},{10,11},{11... | collective-permute-start | bytes 393224 | tf_op jit(solution)/shard_map/ppermute | solution.py:10
  165.6 16.0 %collective-permute-start.2 = (f32[16,16,128]{2,1,0:T(8,128)S(1)}, f32[16,16,128]{2,1,0:T(8,128)S(1)}, u32[]{:S(2)}, u32[]{:S(2)}) collective-permute-start(f32[16,16,128]{2,1,0:T(8,128)S(1)} %dynamic-slice_bitcast_fusion), channel_id=1, source_target_pairs={{0,1},{1,2},{2,3},{3,4},{4,5},{5,6},{6,7},{8,9},{9,10},{10,11},{11... | collective-permute-start | bytes 393224 | tf_op jit(solution)/shard_map/ppermute | solution.py:10
where the time goes:
time: 218 us; the launch traced here: 217 us
  blocking collectives  152 us (70%)
  matrix products  29.4 us (13%)
  local copies, waits for them, and re-layouts  16.2 us (7%)
  other arithmetic  6.73 us (3%)
  between operations  6.34 us (3%)
  starting transfers between devices  5.75 us (3%)
    psum x4, blocking collectives, body(): field_sum = lax.psum(partial_field, 'delay')  93.5 us
    all_gather x3, blocking collectives, body(): newest = lax.all_gather(current, 'src', axis=0, tiled=True)  40.7 us
    dot_general x4, matrix products, body(): jnp.einsum('pab,prb->pra', interaction, picked, precision=lax.Precision.H...  23.8 us
    all_gather x1, blocking collectives, body(): band_state = lax.all_gather(history, 'src', axis=1, tiled=True)  18.1 us
    gather x4, local copies, waits for them, and re-layouts, body(): picked = band_state[holder, pattern[1]]  10.6 us
    ppermute x3, starting transfers between devices, shifted(): return lax.ppermute(x, axis, pairs)  5.75 us
  transfers between devices with their start and end apart: 3, of which 0 were waited for; matrix products, arithmetic and copies ran while one was open for 6% of the time, Pallas kernels for 0%

commit v1 on v0

--- a/solution.py
+++ b/solution.py
@@ -28,7 +28,12 @@
     in_use = (jnp.arange(pair_count, dtype=jnp.int32) < live[0]).astype(jnp.float32)
     row_match = pattern[0][None, :] == jnp.arange(group_blocks, dtype=jnp.int32)[:, None]
     selector = row_match.astype(jnp.float32) * in_use[None, :]
-    band_state = lax.all_gather(history, "src", axis=1, tiled=True)
+    ring = [history]
+    for hop in range(3):
+        ring.append(lax.ppermute(ring[-1], "src", [(dev, (dev + 1) % 4) for dev in range(4)]))
+    band_state = jnp.roll(
+        jnp.concatenate(ring[::-1], axis=1), (lax.axis_index("src") + 1) * ring[0].shape[1], axis=1
+    )
     results = []
     newest = None
     for moment in range(moments):

time: 218 us -> 209 us (0.959)
  blocking collectives: 152 us -> 131 us
  waiting for transfers between devices: 0.01 us -> 7.56 us
  local copies, waits for them, and re-layouts: 16.2 us -> 19.7 us
    all_gather x1 -> x0, blocking collectives: 18.1 us -> none  [body(): band_state = lax.all_gather(history, 'src', axis=1, tiled=True)]
    ppermute x0 -> x3, waiting for transfers between devices: none -> 7.55 us  [body(): lax.ppermute(ring[-1], 'src', [(dev, (dev + 1) % 4) for dev in range(4)])]
    psum x4, blocking collectives: 93.5 us -> 90.7 us  [body(): field_sum = lax.psum(partial_field, 'delay')]
  transfers between devices with their start and end apart: 3 -> 6, of which waited for: 0 -> 2; matrix products, arithmetic and copies ran while one was open for 6% -> 3% of each run, Pallas kernels for 0% -> 0%
where the time goes in v1:
time: 209 us; the launch traced here: 208 us
  blocking collectives  131 us (63%)
  matrix products  29.5 us (14%)
  local copies, waits for them, and re-layouts  19.7 us (9%)
  waiting for transfers between devices  7.56 us (4%)
  starting transfers between devices  7.42 us (4%)
  between operations  6.53 us (3%)
  other arithmetic  6.27 us (3%)
    psum x4, blocking collectives, body(): field_sum = lax.psum(partial_field, 'delay')  90.7 us
    all_gather x3, blocking collectives, body(): newest = lax.all_gather(current, 'src', axis=0, tiled=True)  40.4 us
    dot_general x4, matrix products, body(): jnp.einsum('pab,prb->pra', interaction, picked, precision=lax.Precision.H...  23.8 us
    gather x4, local copies, waits for them, and re-layouts, body(): picked = band_state[holder, pattern[1]]  10.5 us
    ppermute x3, waiting for transfers between devices, body(): lax.ppermute(ring[-1], 'src', [(dev, (dev + 1) % 4) for dev in range(4)])  7.55 us
    ppermute x3, starting transfers between devices, shifted(): return lax.ppermute(x, axis, pairs)  5.76 us
  transfers between devices with their start and end apart: 6, of which 2 were waited for; matrix products, arithmetic and copies ran while one was open for 3% of the time, Pallas kernels for 0%

profile of v1, /device:TPU:4, one launch (start us, length us, event | category | flops | bytes accessed | tf_op | source)
XLA Modules:
  0.0 208.0 jit_solution(6803474781616929520)
XLA Ops:
  0.0 1.6 collective-permute-start
  1.6 1.3 slice_bitcast_fusion.1
  2.8 1.4 fusion.73
  4.3 1.4 fusion.45
  5.8 1.6 collective-permute-done
  8.1 6.0 %collective-permute-done.1 = f32[4,4,16,128]{3,2,1,0:T(8,128)S(1)} collective-permute-done((f32[4,4,16,128]{3,2,1,0:T(8,128)S(1)}, f32[4,4,16,128]{3,2,1,0:T(8,128)S(1)}, u32[]{:S(2)}, u32[]{:S(2)}) %collective-permute-start.1) | collective-permute-done | bytes 131104 | tf_op jit(solution)/shard_map/ppermute | solution.py:33
  21.1 0.9 constant_dynamic-update-slice_fusion.4
  22.1 0.9 constant_dynamic-update-slice_fusion
  23.0 1.0 copy-done.2
  24.8 2.6 %gather_fusion = f32[48,16,128]{2,1,0:T(8,128)} fusion(f32[4,16,16,128]{3,2,1,0:T(8,128)} %constant_dynamic-slice_fusion, s32[48]{0:T(128)S(1)} %get-tuple-element.25), kind=kCustom, calls=%fused_computation | custom fusion | bytes 786816 | tf_op jit(solution)/shard_map/gather | solution.py:48
  27.4 6.0 %fusion.74 = f32[48,16,128]{2,1,0:T(8,128)S(1)} fusion(f32[48,16,128]{2,1,0:T(8,128)} %gather_fusion, f32[48,128,128]{2,1,0:T(8,128)S(1)} %copy-done), kind=kOutput, calls=%fused_computation.130 | convolution fusion | flops 150994944 | bytes 3932160 | tf_op jit(solution)/shard_map/pab,prb->pra/dot_general | solution.py:49
  33.8 22.4 %psum.28 = f32[4,16,128]{2,0,1:T(4,128)S(1)} all-reduce(f32[4,16,128]{2,0,1:T(4,128)S(1)} %fusion.9), channel_id=1, replica_groups=mesh['src'=4,'delay'=8] {'delay'}, use_global_device_ids=true, to_apply=%region_1.2 | all-reduce | flops 8192 | bytes 65536 | tf_op jit(solution)/shard_map/psum | solution.py:56
  56.2 0.9 dynamic-slice_bitcast_fusion.2
  57.1 1.9 collective-permute-start.3
  59.6 13.4 %all_gather.9 = f32[16,16,128]{2,1,0:T(8,128)S(1)} all-gather(f32[4,16,128]{2,1,0:T(8,128)S(1)} %fusion.21), channel_id=1, replica_groups=mesh['src'=4,'delay'=8] {'src'}, dimensions={0}, use_global_device_ids=true | all-gather | bytes 163840 | tf_op jit(solution)/shard_map/all_gather | solution.py:65
  73.7 2.6 %gather_fusion.1 = f32[48,16,128]{2,1,0:T(8,128)} fusion(f32[4,16,16,128]{3,2,1,0:T(8,128)} %bitcast_dynamic-update-slice_fusion.2, s32[48]{0:T(128)S(1)} %get-tuple-element.24), kind=kCustom, calls=%fused_computation.1 | custom fusion | bytes 786816 | tf_op jit(solution)/shard_map/gather | solution.py:48
  76.3 6.0 %fusion.75 = f32[48,16,128]{2,1,0:T(8,128)S(1)} fusion(f32[48,16,128]{2,1,0:T(8,128)} %gather_fusion.1, f32[48,128,128]{2,1,0:T(8,128)S(1)} %copy-done), kind=kOutput, calls=%fused_computation.131 | convolution fusion | flops 150994944 | bytes 3932160 | tf_op jit(solution)/shard_map/pab,prb->pra/dot_general | solution.py:49
  82.2 1.2 fusion.6
  83.4 22.4 %psum.29 = f32[4,16,128]{2,0,1:T(4,128)S(1)} all-reduce(f32[4,16,128]{2,0,1:T(4,128)S(1)} %fusion.6), channel_id=1, replica_groups=mesh['src'=4,'delay'=8] {'delay'}, use_global_device_ids=true, to_apply=%region_4.5 | all-reduce | flops 8192 | bytes 65536 | tf_op jit(solution)/shard_map/psum | solution.py:56
  105.8 0.9 dynamic-slice_bitcast_fusion.1
  106.7 1.9 collective-permute-start.4
  109.2 13.6 %all_gather.10 = f32[16,16,128]{2,1,0:T(8,128)S(1)} all-gather(f32[4,16,128]{2,1,0:T(8,128)S(1)} %fusion.19), channel_id=1, replica_groups=mesh['src'=4,'delay'=8] {'src'}, dimensions={0}, use_global_device_ids=true | all-gather | bytes 163840 | tf_op jit(solution)/shard_map/all_gather | solution.py:65
  123.4 2.6 %gather_fusion.2 = f32[48,16,128]{2,1,0:T(8,128)} fusion(f32[4,16,16,128]{3,2,1,0:T(8,128)} %bitcast_dynamic-update-slice_fusion.1, s32[48]{0:T(128)S(1)} %get-tuple-element.23), kind=kCustom, calls=%fused_computation.2 | custom fusion | bytes 786816 | tf_op jit(solution)/shard_map/gather | solution.py:48
  126.0 6.0 %fusion.76 = f32[48,16,128]{2,1,0:T(8,128)S(1)} fusion(f32[48,16,128]{2,1,0:T(8,128)} %gather_fusion.2, f32[48,128,128]{2,1,0:T(8,128)S(1)} %copy-done), kind=kOutput, calls=%fused_computation.132 | convolution fusion | flops 150994944 | bytes 3932160 | tf_op jit(solution)/shard_map/pab,prb->pra/dot_general | solution.py:49
  132.0 1.0 fusion.3
  133.0 23.0 %psum.30 = f32[4,16,128]{2,0,1:T(4,128)S(1)} all-reduce(f32[4,16,128]{2,0,1:T(4,128)} %fusion.3), channel_id=1, replica_groups=mesh['src'=4,'delay'=8] {'delay'}, use_global_device_ids=true, to_apply=%region_7.8 | all-reduce | flops 8192 | bytes 65536 | tf_op jit(solution)/shard_map/psum | solution.py:56
  156.9 1.9 collective-permute-start.5
  159.4 13.4 %all_gather.11 = f32[16,16,128]{2,1,0:T(8,128)S(1)} all-gather(f32[4,16,128]{2,1,0:T(8,128)S(1)} %fusion.17), channel_id=1, replica_groups=mesh['src'=4,'delay'=8] {'src'}, dimensions={0}, use_global_device_ids=true | all-gather | bytes 163840 | tf_op jit(solution)/shard_map/all_gather | solution.py:65
  173.4 2.6 %gather_fusion.3 = f32[48,16,128]{2,1,0:T(8,128)} fusion(f32[4,16,16,128]{3,2,1,0:T(8,128)} %bitcast_dynamic-update-slice_fusion, s32[48]{0:T(128)S(1)} %get-tuple-element.9), kind=kCustom, calls=%fused_computation.3 | custom fusion | bytes 786816 | tf_op jit(solution)/shard_map/gather | solution.py:48
  176.1 6.0 %fusion.77 = f32[48,16,128]{2,1,0:T(8,128)S(1)} fusion(f32[48,16,128]{2,1,0:T(8,128)} %gather_fusion.3, f32[48,128,128]{2,1,0:T(8,128)S(1)} %copy-done), kind=kOutput, calls=%fused_computation.133 | convolution fusion | flops 150994944 | bytes 3932160 | tf_op jit(solution)/shard_map/pab,prb->pra/dot_general | solution.py:49
  182.0 1.0 fusion
  183.0 23.0 %psum.31 = f32[4,16,128]{2,0,1:T(4,128)S(1)} all-reduce(f32[4,16,128]{2,0,1:T(4,128)} %fusion), channel_id=1, replica_groups=mesh['src'=4,'delay'=8] {'delay'}, use_global_device_ids=true, to_apply=%region_10.11 | all-reduce | flops 8192 | bytes 65536 | tf_op jit(solution)/shard_map/psum | solution.py:56
  (48 shorter events, 9.3 us)
Async XLA Ops:
  0.0 27.4 %copy-start = (f32[48,128,128]{2,1,0:T(8,128)S(1)}, f32[48,128,128]{2,1,0:T(8,128)}, u32[]{:S(2)}) copy-start(f32[48,128,128]{2,1,0:T(8,128)} %param.9) | copy-start | bytes 9437188
  0.0 7.3 %collective-permute-start = (f32[4,4,16,128]{3,2,1,0:T(8,128)}, f32[4,4,16,128]{3,2,1,0:T(8,128)S(1)}, u32[]{:S(2)}, u32[]{:S(2)}) collective-permute-start(f32[4,4,16,128]{3,2,1,0:T(8,128)} %param.7), channel_id=1, source_target_pairs={{0,8},{8,16},{16,24},{24,0},{1,9},{9,17},{17,25},{25,1},{2,10},{10... | collective-permute-start | bytes 393224 | tf_op jit(solution)/shard_map/ppermute | solution.py:33
  7.3 6.8 %collective-permute-start.1 = (f32[4,4,16,128]{3,2,1,0:T(8,128)S(1)}, f32[4,4,16,128]{3,2,1,0:T(8,128)S(1)}, u32[]{:S(2)}, u32[]{:S(2)}) collective-permute-start(f32[4,4,16,128]{3,2,1,0:T(8,128)S(1)} %collective-permute-done), channel_id=1, source_target_pairs={{0,8},{8,16},{16,24},{24,0},{1,9},{9,17},{17,25},{25,1},{2,10},{10... | collective-permute-start | bytes 393224 | tf_op jit(solution)/shard_map/ppermute | solution.py:33
  14.1 6.9 %collective-permute-start.2 = (f32[4,4,16,128]{3,2,1,0:T(8,128)S(1)}, f32[4,4,16,128]{3,2,1,0:T(8,128)S(1)}, u32[]{:S(2)}, u32[]{:S(2)}) collective-permute-start(f32[4,4,16,128]{3,2,1,0:T(8,128)S(1)} %collective-permute-done.1), channel_id=1, source_target_pairs={{0,8},{8,16},{16,24},{24,0},{1,9},{9,17},{17,25},{25,1},{2,10},{10... | collective-permute-start | bytes 393224 | tf_op jit(solution)/shard_map/ppermute | solution.py:33
  22.0 11.4 %copy-start.6 = (s32[48]{0:T(128)S(1)}, s32[48]{0:T(128)}, u32[]{:S(2)}) copy-start(s32[48]{0:T(128)} %get-tuple-element.21) | copy-start | bytes 580
  22.0 11.4 %copy-start.7 = (f32[48]{0:T(128)S(1)}, f32[48]{0:T(128)}, u32[]{:S(2)}) copy-start(f32[48]{0:T(128)} %compare_convert_fusion) | copy-start | bytes 580
  23.0 1.0 copy-start.2
  24.0 35.1 %copy-start.5 = (f32[1,4,16,128]{3,2,1,0:T(8,128)S(1)}, f32[1,4,16,128]{3,2,1,0:T(8,128)}, u32[]{:S(2)}) copy-start(f32[1,4,16,128]{3,2,1,0:T(8,128)} %get-tuple-element.20) | copy-start | bytes 98308
  24.0 35.1 %copy-start.1 = (f32[4,128,128]{2,1,0:T(8,128)S(1)}, f32[4,128,128]{2,1,0:T(8,128)}, u32[]{:S(2)}) copy-start(f32[4,128,128]{2,1,0:T(8,128)} %param.12) | copy-start | bytes 786436
  57.1 15.9 %collective-permute-start.3 = (f32[16,16,128]{2,1,0:T(8,128)S(1)}, f32[16,16,128]{2,1,0:T(8,128)S(1)}, u32[]{:S(2)}, u32[]{:S(2)}) collective-permute-start(f32[16,16,128]{2,1,0:T(8,128)S(1)} %dynamic-slice_bitcast_fusion.2), channel_id=1, source_target_pairs={{0,1},{1,2},{2,3},{3,4},{4,5},{5,6},{6,7},{8,9},{9,10},{10,11},{11... | collective-permute-start | bytes 393224 | tf_op jit(solution)/shard_map/ppermute | solution.py:10
  59.1 49.5 %copy-start.4 = (f32[1,4,16,128]{3,2,1,0:T(8,128)S(1)}, f32[1,4,16,128]{3,2,1,0:T(8,128)}, u32[]{:S(2)}) copy-start(f32[1,4,16,128]{3,2,1,0:T(8,128)} %get-tuple-element.19) | copy-start | bytes 98308
  82.2 49.8 %copy-start.8 = (f32[48]{0:T(128)S(1)}, f32[48]{0:T(128)}, u32[]{:S(2)}) copy-start(f32[48]{0:T(128)} %compare_convert_fusion) | copy-start | bytes 580
  106.7 16.1 %collective-permute-start.4 = (f32[16,16,128]{2,1,0:T(8,128)S(1)}, f32[16,16,128]{2,1,0:T(8,128)S(1)}, u32[]{:S(2)}, u32[]{:S(2)}) collective-permute-start(f32[16,16,128]{2,1,0:T(8,128)S(1)} %dynamic-slice_bitcast_fusion.1), channel_id=1, source_target_pairs={{0,1},{1,2},{2,3},{3,4},{4,5},{5,6},{6,7},{8,9},{9,10},{10,11},{11... | collective-permute-start | bytes 393224 | tf_op jit(solution)/shard_map/ppermute | solution.py:10
  108.7 50.2 %copy-start.3 = (f32[1,4,16,128]{3,2,1,0:T(8,128)S(1)}, f32[1,4,16,128]{3,2,1,0:T(8,128)}, u32[]{:S(2)}) copy-start(f32[1,4,16,128]{3,2,1,0:T(8,128)} %get-tuple-element.18) | copy-start | bytes 98308
  156.9 15.9 %collective-permute-start.5 = (f32[16,16,128]{2,1,0:T(8,128)S(1)}, f32[16,16,128]{2,1,0:T(8,128)S(1)}, u32[]{:S(2)}, u32[]{:S(2)}) collective-permute-start(f32[16,16,128]{2,1,0:T(8,128)S(1)} %dynamic-slice_bitcast_fusion), channel_id=1, source_target_pairs={{0,1},{1,2},{2,3},{3,4},{4,5},{5,6},{6,7},{8,9},{9,10},{10,11},{11... | collective-permute-start | bytes 393224 | tf_op jit(solution)/shard_map/ppermute | solution.py:10
